TPU v7x, 128 devices: a whole 4x4x4 slice. The times are simulated.
128 devices in a mesh: ens: 8 (over z_lo, y), lat: 16 (over x, z_hi, core).
Axes of the slice: x: 4, y: 4, z: 4 (z_hi: 2, z_lo: 2; z = z_hi * 2 + z_lo), core: 2. Of those that a mesh axis runs over, the one named last changes fastest.
Arguments:
- prediction_array: float32 [16, 16, 128, 1440], P('ens', None, 'lat'), may hold values from -6 to 6
- verifying_analysis: float32 [16, 128, 1440], P('ens', 'lat'), may hold values from -6 to 6
- variable_penalty_factor: float32 [16], replicated, may hold values from 0.25 to 4
Outputs:
- field_grad: float32 [16, 16, 128, 1440], P('ens', None, 'lat')
All inputs are finite; a program needn't handle non-finite values.
Results may differ from a plain program's by a relative error of at most 0.00002.
Values sent between devices are 32-bit elements; how exact they have to be, the bound alone decides.
No kernel may reach another device: no remote copies, remote signals or barrier semaphores. Data moves between devices by JAX's collectives and lax.ppermute only.
A program may use at most 64 MiB of HBM per device.

v0:
```python
import jax
import jax.numpy as jnp
from jax import lax
from jax.sharding import PartitionSpec as P

COARSE = 3


def with_halo(block, sides, width):
    for axis, dim in sides:
        count = lax.axis_size(axis)
        forward = [(i, i + 1) for i in range(count - 1)]
        backward = [(target, source) for source, target in forward]
        low = lax.ppermute(
            lax.slice_in_dim(block, block.shape[dim] - width, None, axis=dim), axis, forward
        )
        high = lax.ppermute(lax.slice_in_dim(block, 0, width, axis=dim), axis, backward)
        block = jnp.concatenate([low, block, high], axis=dim)
    return block


def slope(differ):
    return differ * lax.rsqrt(differ * differ + 0.01)


def normal_kernel_smoother(extended, first_row, lat_total):
    along = 0.25 * extended[:, :-2] + 0.5 * extended[:, 1:-1] + 0.25 * extended[:, 2:]
    result = 0.25 * jnp.roll(along, 1, -1) + 0.5 * along + 0.25 * jnp.roll(along, -1, -1)
    row_ids = first_row + 1 + jnp.arange(result.shape[1])
    inside = (row_ids >= 0) & (row_ids < lat_total)
    return jnp.where(inside[None, :, None], result, 0.0)


def near_forward(field, lat_start, lat_total):
    extended = with_halo(field, (("lat", 1),), 1)
    return normal_kernel_smoother(extended, lat_start - 1, lat_total)


def near_back(field, lat_start, lat_total):
    extended = with_halo(field, (("lat", 1),), 1)
    return normal_kernel_smoother(extended, lat_start - 1, lat_total)


def forward_blur(stacked_fields, lat_start, lat_total):
    fine_part = near_forward(stacked_fields, lat_start, lat_total)
    level = fine_part
    for repeat in range(COARSE - 1):
        level = near_forward(level, lat_start, lat_total)
    return (fine_part, level)


def back_blur(fine_grad, coarse_grad, lat_start, lat_total):
    level = coarse_grad
    for repeat in range(COARSE - 1):
        level = near_back(level, lat_start, lat_total)
    level = level + fine_grad
    return near_back(level, lat_start, lat_total)


def couple_derivative(smooth_fc, smooth_obs, penalty_factor):
    count = smooth_fc.shape[0]

    def single(member):
        return jnp.sum(slope(member[None] - smooth_fc), axis=0)

    pulls = lax.map(single, smooth_fc)
    return penalty_factor * (slope(smooth_fc - smooth_obs[None]) - 0.95 / (count - 1) * pulls)


def body(prediction_array, verifying_analysis, variable_penalty_factor):
    ensemble_size, variable_number, parallel_number, meridian_number = prediction_array.shape
    group_size = verifying_analysis.shape[0]
    ens_index = lax.axis_index("ens")
    lat_start = lax.axis_index("lat") * parallel_number
    lat_total = lax.axis_size("lat") * parallel_number
    row_ids = (lat_start + jnp.arange(parallel_number)).astype(jnp.float32)
    degrees = 0.25 * (row_ids - (lat_total - 1) / 2.0)
    lat_weight = jnp.cos(jnp.deg2rad(degrees))
    chan_weight = lax.dynamic_slice_in_dim(
        variable_penalty_factor, ens_index * group_size, group_size
    )
    penalty_factor = chan_weight[:, None, None] * lat_weight[None, :, None]
    divide_parallels = ensemble_size * variable_number
    stacked_fields = jnp.concatenate(
        [
            prediction_array.reshape(divide_parallels, parallel_number, meridian_number),
            verifying_analysis,
        ],
        0,
    )
    fine_all, coarse_all = forward_blur(stacked_fields, lat_start, lat_total)
    fine_mine = fine_all[:divide_parallels].reshape(
        ensemble_size, variable_number, parallel_number, meridian_number
    )
    coarse_mine = coarse_all[:divide_parallels].reshape(
        ensemble_size, variable_number, parallel_number, meridian_number
    )
    fine_group, coarse_group = (
        lax.all_to_all(fine_mine, "ens", split_axis=1, concat_axis=0, tiled=True),
        lax.all_to_all(coarse_mine, "ens", split_axis=1, concat_axis=0, tiled=True),
    )
    sharp_derivative = couple_derivative(fine_group, fine_all[divide_parallels:], penalty_factor)
    grad_coarse = couple_derivative(coarse_group, coarse_all[divide_parallels:], penalty_factor)
    fine_back, coarse_back = (
        lax.all_to_all(sharp_derivative, "ens", split_axis=0, concat_axis=1, tiled=True),
        lax.all_to_all(grad_coarse, "ens", split_axis=0, concat_axis=1, tiled=True),
    )
    result = back_blur(
        fine_back.reshape(divide_parallels, parallel_number, meridian_number),
        coarse_back.reshape(divide_parallels, parallel_number, meridian_number),
        lat_start,
        lat_total,
    )
    return result.reshape(ensemble_size, variable_number, parallel_number, meridian_number)


def solution(mesh):
    placed = (P("ens", None, "lat", None), P("ens", "lat", None), P())
    return jax.shard_map(
        body, mesh=mesh, in_specs=placed, out_specs=P("ens", None, "lat", None), check_vma=False
    )
```

profile of v0, /device:TPU:1, one launch (start us, length us, event | category | flops | bytes accessed | tf_op | source)
XLA Modules:
  0.0 197.1 jit_solution(5415008089006157320)
XLA Ops:
  0.0 2.4 %fusion.44 = (f32[34,1,1440]{2,1,0:T(1,128)S(1)}, f32[34,1,1440]{2,1,0:T(1,128)S(1)}) fusion(f32[32,8,1440]{2,1,0:T(8,128)} %bitcast.46, f32[2,8,1440]{2,1,0:T(8,128)} %param.8), kind=kLoop, calls=%fused_computation.83 | loop fusion | flops 97920 | bytes 1958400 | tf_op jit(solution)/shard_map/concatenate | solution.py:84
  2.4 6.9 %collective-permute-start = (f32[34,1,1440]{2,1,0:T(1,128)S(1)}, f32[34,1,1440]{2,1,0:T(1,128)S(1)}, u32[]{:S(2)}, u32[]{:S(2)}) collective-permute-start(f32[34,1,1440]{2,1,0:T(1,128)S(1)} %get-tuple-element.69), channel_id=1, source_target_pairs={{0,1},{1,2},{2,3},{3,4},{4,5},{5,6},{6,7},{7,8},{8,9},{9,10},{10,1... | collective-permute-start | bytes 587528 | tf_op jit(solution)/shard_map/ppermute | solution.py:14
  12.0 5.9 %collective-permute-done.1 = f32[34,1,1440]{2,1,0:T(1,128)S(1)} collective-permute-done((f32[34,1,1440]{2,1,0:T(1,128)S(1)}, f32[34,1,1440]{2,1,0:T(1,128)S(1)}, u32[]{:S(2)}, u32[]{:S(2)}) %collective-permute-start.1) | collective-permute-done | bytes 195872 | tf_op jit(solution)/shard_map/ppermute | solution.py:17
  22.3 2.4 %collective-permute-start.3 = (f32[34,1,1440]{2,1,0:T(1,128)S(1)}, f32[34,1,1440]{2,1,0:T(1,128)S(1)}, u32[]{:S(2)}, u32[]{:S(2)}) collective-permute-start(f32[34,1,1440]{2,1,0:T(1,128)S(1)} %get-tuple-element.64), channel_id=1, source_target_pairs={{1,0},{2,1},{3,2},{4,3},{5,4},{6,5},{7,6},{8,7},{9,8},{10,9},{11,1... | collective-permute-start | bytes 587528 | tf_op jit(solution)/shard_map/ppermute | solution.py:17
  25.0 5.9 %collective-permute-done.3 = f32[34,1,1440]{2,1,0:T(1,128)S(1)} collective-permute-done((f32[34,1,1440]{2,1,0:T(1,128)S(1)}, f32[34,1,1440]{2,1,0:T(1,128)S(1)}, u32[]{:S(2)}, u32[]{:S(2)}) %collective-permute-start.3) | collective-permute-done | bytes 195872 | tf_op jit(solution)/shard_map/ppermute | solution.py:17
  32.4 2.3 %fusion.18 = f32[34,8,1440]{2,1,0:T(8,128)S(1)} fusion(f32[34,8,1439]{2,1,0:T(8,128)S(1)} %get-tuple-element.60, f32[34,8,1]{2,1,0:T(8,128)S(1)} %get-tuple-element.62, f32[34,8,1]{2,1,0:T(8,128)S(1)} %get-tuple-element.61, f32[34,8,1439]{2,1,0:T(8,128)S(1)} %get-tuple-element.59, pred[8]{0:T(512)(128)(4,1)S(1)} %compare_and_fusion, ...), kind=kLoop, calls=%fused_computation.38 | loop fusion | flops 5875200 | bytes 6658568 | tf_op jit(solution)/shard_map/jit(_where)/select_n | solution.py:31
  37.6 2.4 %collective-permute-start.5 = (f32[34,1,1440]{2,1,0:T(1,128)}, f32[34,1,1440]{2,1,0:T(1,128)}, u32[]{:S(2)}, u32[]{:S(2)}) collective-permute-start(f32[34,1,1440]{2,1,0:T(1,128)} %get-tuple-element.58), channel_id=1, source_target_pairs={{1,0},{2,1},{3,2},{4,3},{5,4},{6,5},{7,6},{8,7},{9,8},{10,9},{11,1... | collective-permute-start | bytes 587528 | tf_op jit(solution)/shard_map/ppermute | solution.py:17
  42.1 4.6 %all-to-all-start.2 = ((f32[2,16,8,1440]{3,2,0,1:T(8,128)}), f32[2,16,8,1440]{3,2,0,1:T(8,128)S(1)}, u32[]{:S(2)}, u32[]{:S(2)}) async-start(f32[2,16,8,1440]{3,2,0,1:T(8,128)} %copy.24), calls=%async_computation.2 | async-start | bytes 3145728 | tf_op jit(solution)/shard_map/all_to_all | solution.py:99
  49.2 2.3 %fusion.21 = f32[34,8,1440]{2,1,0:T(8,128)S(1)} fusion(f32[34,8,1439]{2,1,0:T(8,128)S(1)} %get-tuple-element.54, f32[34,8,1]{2,1,0:T(8,128)S(1)} %get-tuple-element.56, f32[34,8,1]{2,1,0:T(8,128)S(1)} %get-tuple-element.55, f32[34,8,1439]{2,1,0:T(8,128)S(1)} %get-tuple-element.53, pred[8]{0:T(512)(128)(4,1)S(1)} %compare_and_fusion, ...), kind=kLoop, calls=%fused_computation.43 | loop fusion | flops 5875200 | bytes 6658568 | tf_op jit(solution)/shard_map/jit(_where)/select_n | solution.py:31
  54.0 14.5 %all-to-all-done.2 = f32[2,16,8,1440]{3,2,0,1:T(8,128)S(1)} async-done(((f32[2,16,8,1440]{3,2,0,1:T(8,128)}), f32[2,16,8,1440]{3,2,0,1:T(8,128)S(1)}, u32[]{:S(2)}, u32[]{:S(2)}) %all-to-all-start.2) | async-done | bytes 1474592 | tf_op jit(solution)/shard_map/all_to_all | solution.py:99
  69.7 5.9 %all-to-all-start = ((f32[2,16,8,1440]{3,2,0,1:T(8,128)}), f32[2,16,8,1440]{3,2,0,1:T(8,128)S(1)}, u32[]{:S(2)}, u32[]{:S(2)}) async-start(f32[2,16,8,1440]{3,2,0,1:T(8,128)} %copy.20), calls=%async_computation | async-start | bytes 3145728 | tf_op jit(solution)/shard_map/all_to_all | solution.py:100
  78.5 15.7 %while.21 = (s32[]{:T(128)}, f32[16,2,8,1440]{3,2,1,0:T(8,128)}, f32[16,2,8,1440]{3,2,1,0:T(8,128)S(1)}, s32[]{:T(128)}) while((s32[]{:T(128)}, f32[16,2,8,1440]{3,2,1,0:T(8,128)}, f32[16,2,8,1440]{3,2,1,0:T(8,128)S(1)}, s32[]{:T(128)}) %tuple.56), condition=%wide.region_5.6_spmd, body=%wide.region_3.5_spmd.sunk | while | flops 1820162 | bytes 2034233 | solution.py:66
  94.2 2.9 %all-to-all-done = f32[2,16,8,1440]{3,2,0,1:T(8,128)S(1)} async-done(((f32[2,16,8,1440]{3,2,0,1:T(8,128)}), f32[2,16,8,1440]{3,2,0,1:T(8,128)S(1)}, u32[]{:S(2)}, u32[]{:S(2)}) %all-to-all-start) | async-done | bytes 1474592 | tf_op jit(solution)/shard_map/all_to_all | solution.py:100
  101.2 15.7 %while.20 = (s32[]{:T(128)}, f32[16,2,8,1440]{3,2,1,0:T(8,128)}, f32[16,2,8,1440]{3,2,1,0:T(8,128)S(1)}, s32[]{:T(128)}) while((s32[]{:T(128)}, f32[16,2,8,1440]{3,2,1,0:T(8,128)}, f32[16,2,8,1440]{3,2,1,0:T(8,128)S(1)}, s32[]{:T(128)}) %tuple.57), condition=%wide.region_2.3_spmd, body=%wide.region_0.2_spmd.sunk | while | flops 1820162 | bytes 2034233 | solution.py:66
  116.8 3.9 %subtract_multiply_fusion = (f32[16,2,8,1440]{3,2,1,0:T(8,128)}, f32[16,2,8,1440]{3,2,1,0:T(8,128)S(1)}) fusion(f32[16,2,8,1440]{3,2,1,0:T(8,128)} %get-tuple-element.40, f32[2,8,1440]{2,1,0:T(8,128)S(1)} %slice-done, f32[2,8]{1,0:T(2,128)S(1)} %copy-done.7, f32[8,2,2,8,1440]{4,3,2,1,0:T(8,128)S(1)} %bitcast.40, f32[16,2,8,1440]{3,2,1,0:T(8,128)} %get-tuple-element.39, ...), kind=kLoop, calls=%fused_computation.79 | loop fusion | flops 5160960 | bytes 9031744 | tf_op jit(solution)/shard_map/mul | solution.py:67
  120.7 22.6 %all_to_all.66 = f32[16,2,8,1440]{3,2,1,0:T(8,128)S(1)} all-to-all(f32[16,2,8,1440]{3,2,1,0:T(8,128)S(1)} %get-tuple-element.90), channel_id=1, replica_groups=mesh['ens'=8,'lat'=16] {'ens'}, dimensions={0} | all-to-all | bytes 2949120 | tf_op jit(solution)/shard_map/all_to_all | solution.py:106
  143.7 5.8 %collective-permute-start.6 = (f32[32,1,1440]{2,1,0:T(1,128)S(1)}, f32[32,1,1440]{2,1,0:T(1,128)S(1)}, u32[]{:S(2)}, u32[]{:S(2)}) collective-permute-start(f32[32,1,1440]{2,1,0:T(1,128)S(1)} %get-tuple-element.87), channel_id=1, source_target_pairs={{0,1},{1,2},{2,3},{3,4},{4,5},{5,6},{6,7},{7,8},{8,9},{9,10},{10,1... | collective-permute-start | bytes 552968 | tf_op jit(solution)/shard_map/ppermute | solution.py:14
  151.5 4.3 %all-to-all-start.3 = ((f32[16,2,8,1440]{3,2,1,0:T(8,128)}), f32[16,2,8,1440]{3,2,1,0:T(8,128)}, u32[]{:S(2)}, u32[]{:S(2)}) async-start(f32[16,2,8,1440]{3,2,1,0:T(8,128)} %get-tuple-element.89), calls=%async_computation.3 | async-start | bytes 3145728 | tf_op jit(solution)/shard_map/all_to_all | solution.py:105
  155.8 3.6 %collective-permute-done.7 = f32[32,1,1440]{2,1,0:T(1,128)S(1)} collective-permute-done((f32[32,1,1440]{2,1,0:T(1,128)S(1)}, f32[32,1,1440]{2,1,0:T(1,128)S(1)}, u32[]{:S(2)}, u32[]{:S(2)}) %collective-permute-start.7) | collective-permute-done | bytes 184352 | tf_op jit(solution)/shard_map/ppermute | solution.py:17
  164.3 2.4 %collective-permute-start.9 = (f32[32,1,1440]{2,1,0:T(1,128)S(1)}, f32[32,1,1440]{2,1,0:T(1,128)S(1)}, u32[]{:S(2)}, u32[]{:S(2)}) collective-permute-start(f32[32,1,1440]{2,1,0:T(1,128)S(1)} %get-tuple-element.82), channel_id=1, source_target_pairs={{1,0},{2,1},{3,2},{4,3},{5,4},{6,5},{7,6},{8,7},{9,8},{10,9},{11,1... | collective-permute-start | bytes 552968 | tf_op jit(solution)/shard_map/ppermute | solution.py:17
  166.7 9.8 %all-to-all-done.3 = f32[16,2,8,1440]{3,2,1,0:T(8,128)} async-done(((f32[16,2,8,1440]{3,2,1,0:T(8,128)}), f32[16,2,8,1440]{3,2,1,0:T(8,128)}, u32[]{:S(2)}, u32[]{:S(2)}) %all-to-all-start.3) | async-done | bytes 1474592 | tf_op jit(solution)/shard_map/all_to_all | solution.py:105
  181.1 3.6 %collective-permute-start.10 = (f32[32,1,1440]{2,1,0:T(1,128)S(1)}, f32[32,1,1440]{2,1,0:T(1,128)S(1)}, u32[]{:S(2)}, u32[]{:S(2)}) collective-permute-start(f32[32,1,1440]{2,1,0:T(1,128)S(1)} %get-tuple-element.75), channel_id=1, source_target_pairs={{0,1},{1,2},{2,3},{3,4},{4,5},{5,6},{6,7},{7,8},{8,9},{9,10},{10,1... | collective-permute-start | bytes 552968 | tf_op jit(solution)/shard_map/ppermute | solution.py:14
  187.3 5.9 %collective-permute-done.11 = f32[32,1,1440]{2,1,0:T(1,128)S(1)} collective-permute-done((f32[32,1,1440]{2,1,0:T(1,128)S(1)}, f32[32,1,1440]{2,1,0:T(1,128)S(1)}, u32[]{:S(2)}, u32[]{:S(2)}) %collective-permute-start.11) | collective-permute-done | bytes 184352 | tf_op jit(solution)/shard_map/ppermute | solution.py:17
  194.7 2.4 %fusion.43 = f32[32,8,1440]{2,1,0:T(8,128)} fusion(f32[32,8,1439]{2,1,0:T(8,128)S(1)} %get-tuple-element.72, f32[32,8,1]{2,1,0:T(8,128)S(1)} %get-tuple-element.74, f32[32,8,1]{2,1,0:T(8,128)S(1)} %get-tuple-element.73, f32[32,8,1439]{2,1,0:T(8,128)S(1)} %get-tuple-element.71, pred[8]{0:T(512)(128)(4,1)S(1)} %compare_and_fusion, ...), kind=kLoop, calls=%fused_computation.77 | loop fusion | flops 5529600 | bytes 6266888 | tf_op jit(solution)/shard_map/jit(_where)/select_n | solution.py:31
  (172 shorter events, 73.7 us)
Async XLA Ops:
  0.0 17.9 %copy-start.2 = (f32[2,16,8,1440]{3,2,1,0:T(8,128)S(1)}, f32[2,16,8,1440]{3,2,1,0:T(8,128)}, u32[]{:S(2)}) copy-start(f32[2,16,8,1440]{3,2,1,0:T(8,128)} %param.7) | copy-start | bytes 4423684
  0.0 17.9 %copy-start.6 = (f32[2,8,1440]{2,1,0:T(8,128)S(1)}, f32[2,8,1440]{2,1,0:T(8,128)}, u32[]{:S(2)}) copy-start(f32[2,8,1440]{2,1,0:T(8,128)} %param.8) | copy-start | bytes 276484
  2.4 9.6 %collective-permute-start = (f32[34,1,1440]{2,1,0:T(1,128)S(1)}, f32[34,1,1440]{2,1,0:T(1,128)S(1)}, u32[]{:S(2)}, u32[]{:S(2)}) collective-permute-start(f32[34,1,1440]{2,1,0:T(1,128)S(1)} %get-tuple-element.69), channel_id=1, source_target_pairs={{0,1},{1,2},{2,3},{3,4},{4,5},{5,6},{6,7},{7,8},{8,9},{9,10},{10,1... | collective-permute-start | bytes 587528 | tf_op jit(solution)/shard_map/ppermute | solution.py:14
  9.3 8.6 %collective-permute-start.1 = (f32[34,1,1440]{2,1,0:T(1,128)S(1)}, f32[34,1,1440]{2,1,0:T(1,128)S(1)}, u32[]{:S(2)}, u32[]{:S(2)}) collective-permute-start(f32[34,1,1440]{2,1,0:T(1,128)S(1)} %get-tuple-element.70), channel_id=1, source_target_pairs={{1,0},{2,1},{3,2},{4,3},{5,4},{6,5},{7,6},{8,7},{9,8},{10,9},{11,1... | collective-permute-start | bytes 587528 | tf_op jit(solution)/shard_map/ppermute | solution.py:17
  19.5 5.2 %copy-start.8 = (f32[16]{0:T(128)S(1)}, f32[16]{0:T(128)}, u32[]{:S(2)}) copy-start(f32[16]{0:T(128)} %param.9) | copy-start | bytes 196
  20.1 20.8 %copy-start = (f32[34,8,1440]{2,1,0:T(8,128)}, f32[34,8,1440]{2,1,0:T(8,128)S(1)}, u32[]{:S(2)}) copy-start(f32[34,8,1440]{2,1,0:T(8,128)S(1)} %fusion.15) | copy-start | bytes 4700164
  20.3 4.7 %collective-permute-start.2 = (f32[34,1,1440]{2,1,0:T(1,128)S(1)}, f32[34,1,1440]{2,1,0:T(1,128)S(1)}, u32[]{:S(2)}, u32[]{:S(2)}) collective-permute-start(f32[34,1,1440]{2,1,0:T(1,128)S(1)} %get-tuple-element.63), channel_id=1, source_target_pairs={{0,1},{1,2},{2,3},{3,4},{4,5},{5,6},{6,7},{7,8},{8,9},{9,10},{10,1... | collective-permute-start | bytes 587528 | tf_op jit(solution)/shard_map/ppermute | solution.py:14
  22.3 8.6 %collective-permute-start.3 = (f32[34,1,1440]{2,1,0:T(1,128)S(1)}, f32[34,1,1440]{2,1,0:T(1,128)S(1)}, u32[]{:S(2)}, u32[]{:S(2)}) collective-permute-start(f32[34,1,1440]{2,1,0:T(1,128)S(1)} %get-tuple-element.64), channel_id=1, source_target_pairs={{1,0},{2,1},{3,2},{4,3},{5,4},{6,5},{7,6},{8,7},{9,8},{10,9},{11,1... | collective-permute-start | bytes 587528 | tf_op jit(solution)/shard_map/ppermute | solution.py:17
  35.7 11.0 %collective-permute-start.4 = (f32[34,1,1440]{2,1,0:T(1,128)}, f32[34,1,1440]{2,1,0:T(1,128)S(1)}, u32[]{:S(2)}, u32[]{:S(2)}) collective-permute-start(f32[34,1,1440]{2,1,0:T(1,128)} %get-tuple-element.57), channel_id=1, source_target_pairs={{0,1},{1,2},{2,3},{3,4},{4,5},{5,6},{6,7},{7,8},{8,9},{9,10},{10,1... | collective-permute-start | bytes 587528 | tf_op jit(solution)/shard_map/ppermute | solution.py:14
  37.6 9.1 %collective-permute-start.5 = (f32[34,1,1440]{2,1,0:T(1,128)}, f32[34,1,1440]{2,1,0:T(1,128)}, u32[]{:S(2)}, u32[]{:S(2)}) collective-permute-start(f32[34,1,1440]{2,1,0:T(1,128)} %get-tuple-element.58), channel_id=1, source_target_pairs={{1,0},{2,1},{3,2},{4,3},{5,4},{6,5},{7,6},{8,7},{9,8},{10,9},{11,1... | collective-permute-start | bytes 587528 | tf_op jit(solution)/shard_map/ppermute | solution.py:17
  42.1 26.4 %all-to-all-start.2 = ((f32[2,16,8,1440]{3,2,0,1:T(8,128)}), f32[2,16,8,1440]{3,2,0,1:T(8,128)S(1)}, u32[]{:S(2)}, u32[]{:S(2)}) async-start(f32[2,16,8,1440]{3,2,0,1:T(8,128)} %copy.24), calls=%async_computation.2 | async-start | bytes 3145728 | tf_op jit(solution)/shard_map/all_to_all | solution.py:99
  51.5 1.2 copy-start.1
  69.7 27.4 %all-to-all-start = ((f32[2,16,8,1440]{3,2,0,1:T(8,128)}), f32[2,16,8,1440]{3,2,0,1:T(8,128)S(1)}, u32[]{:S(2)}, u32[]{:S(2)}) async-start(f32[2,16,8,1440]{3,2,0,1:T(8,128)} %copy.20), calls=%async_computation | async-start | bytes 3145728 | tf_op jit(solution)/shard_map/all_to_all | solution.py:100
  97.1 1.2 copy-start.3
  101.2 15.7 %slice-start = ((f32[34,8,1440]{2,1,0:T(8,128)}), f32[2,8,1440]{2,1,0:T(8,128)S(1)}, s32[]{:S(2)}) async-start(f32[34,8,1440]{2,1,0:T(8,128)} %copy-done), calls=%async_computation.4 | async-start | bytes 196608 | tf_op jit(solution)/shard_map/slice | solution.py:102
  101.2 15.7 %slice-start.1 = ((f32[34,8,1440]{2,1,0:T(8,128)}), f32[2,8,1440]{2,1,0:T(8,128)S(1)}, s32[]{:S(2)}) async-start(f32[34,8,1440]{2,1,0:T(8,128)} %copy-done.1), calls=%async_computation.5 | async-start | bytes 196608 | tf_op jit(solution)/shard_map/slice | solution.py:103
  101.2 15.7 %copy-start.7 = (f32[2,8]{1,0:T(2,128)S(1)}, f32[2,8]{1,0:T(2,128)}, u32[]{:S(2)}) copy-start(f32[2,8]{1,0:T(2,128)} %broadcast_multiply_fusion) | copy-start | bytes 196
  143.7 12.1 %collective-permute-start.6 = (f32[32,1,1440]{2,1,0:T(1,128)S(1)}, f32[32,1,1440]{2,1,0:T(1,128)S(1)}, u32[]{:S(2)}, u32[]{:S(2)}) collective-permute-start(f32[32,1,1440]{2,1,0:T(1,128)S(1)} %get-tuple-element.87), channel_id=1, source_target_pairs={{0,1},{1,2},{2,3},{3,4},{4,5},{5,6},{6,7},{7,8},{8,9},{9,10},{10,1... | collective-permute-start | bytes 552968 | tf_op jit(solution)/shard_map/ppermute | solution.py:14
  149.5 9.9 %collective-permute-start.7 = (f32[32,1,1440]{2,1,0:T(1,128)S(1)}, f32[32,1,1440]{2,1,0:T(1,128)S(1)}, u32[]{:S(2)}, u32[]{:S(2)}) collective-permute-start(f32[32,1,1440]{2,1,0:T(1,128)S(1)} %get-tuple-element.88), channel_id=1, source_target_pairs={{1,0},{2,1},{3,2},{4,3},{5,4},{6,5},{7,6},{8,7},{9,8},{10,9},{11,1... | collective-permute-start | bytes 552968 | tf_op jit(solution)/shard_map/ppermute | solution.py:17
  151.5 25.1 %all-to-all-start.3 = ((f32[16,2,8,1440]{3,2,1,0:T(8,128)}), f32[16,2,8,1440]{3,2,1,0:T(8,128)}, u32[]{:S(2)}, u32[]{:S(2)}) async-start(f32[16,2,8,1440]{3,2,1,0:T(8,128)} %get-tuple-element.89), calls=%async_computation.3 | async-start | bytes 3145728 | tf_op jit(solution)/shard_map/all_to_all | solution.py:105
  162.4 15.7 %collective-permute-start.8 = (f32[32,1,1440]{2,1,0:T(1,128)S(1)}, f32[32,1,1440]{2,1,0:T(1,128)S(1)}, u32[]{:S(2)}, u32[]{:S(2)}) collective-permute-start(f32[32,1,1440]{2,1,0:T(1,128)S(1)} %get-tuple-element.81), channel_id=1, source_target_pairs={{0,1},{1,2},{2,3},{3,4},{4,5},{5,6},{6,7},{7,8},{8,9},{9,10},{10,1... | collective-permute-start | bytes 552968 | tf_op jit(solution)/shard_map/ppermute | solution.py:14
  164.3 13.8 %collective-permute-start.9 = (f32[32,1,1440]{2,1,0:T(1,128)S(1)}, f32[32,1,1440]{2,1,0:T(1,128)S(1)}, u32[]{:S(2)}, u32[]{:S(2)}) collective-permute-start(f32[32,1,1440]{2,1,0:T(1,128)S(1)} %get-tuple-element.82), channel_id=1, source_target_pairs={{1,0},{2,1},{3,2},{4,3},{5,4},{6,5},{7,6},{8,7},{9,8},{10,9},{11,1... | collective-permute-start | bytes 552968 | tf_op jit(solution)/shard_map/ppermute | solution.py:17
  181.1 6.2 %collective-permute-start.10 = (f32[32,1,1440]{2,1,0:T(1,128)S(1)}, f32[32,1,1440]{2,1,0:T(1,128)S(1)}, u32[]{:S(2)}, u32[]{:S(2)}) collective-permute-start(f32[32,1,1440]{2,1,0:T(1,128)S(1)} %get-tuple-element.75), channel_id=1, source_target_pairs={{0,1},{1,2},{2,3},{3,4},{4,5},{5,6},{6,7},{7,8},{8,9},{9,10},{10,1... | collective-permute-start | bytes 552968 | tf_op jit(solution)/shard_map/ppermute | solution.py:14
  184.8 8.5 %collective-permute-start.11 = (f32[32,1,1440]{2,1,0:T(1,128)S(1)}, f32[32,1,1440]{2,1,0:T(1,128)S(1)}, u32[]{:S(2)}, u32[]{:S(2)}) collective-permute-start(f32[32,1,1440]{2,1,0:T(1,128)S(1)} %get-tuple-element.76), channel_id=1, source_target_pairs={{1,0},{2,1},{3,2},{4,3},{5,4},{6,5},{7,6},{8,7},{9,8},{10,9},{11,1... | collective-permute-start | bytes 552968 | tf_op jit(solution)/shard_map/ppermute | solution.py:17
  (2 other events, 2.0 us)
where the time goes:
time: 201 us; the launch traced here: 197 us
  starting transfers between devices  50.2 us (25%)
  waiting for transfers between devices  50 us (25%)
  local copies, waits for them, and re-layouts  40.8 us (20%)
  other arithmetic  32.9 us (16%)
  blocking collectives  22.6 us (11%)
    all_to_all x1, blocking collectives, body(): lax.all_to_all(grad_coarse, 'ens', split_axis=0, concat_axis=1, tiled=True)  22.6 us
    ppermute x6, starting transfers between devices, with_halo(): lax.ppermute(lax.slice_in_dim(block, block.shape[dim] - width, None, axis...  22.1 us
    ppermute x6, waiting for transfers between devices, with_halo(): lax.ppermute(lax.slice_in_dim(block, 0, width, axis=dim), axis, backward)  21.3 us
    dynamic_update_slice x32, local copies, waits for them, and re-layouts, couple_derivative(): pulls = lax.map(single, smooth_fc)  20.9 us
    all_to_all x1, waiting for transfers between devices, body(): lax.all_to_all(fine_mine, 'ens', split_axis=1, concat_axis=0, tiled=True)  14.5 us
    ppermute x6, starting transfers between devices, with_halo(): lax.ppermute(lax.slice_in_dim(block, 0, width, axis=dim), axis, backward)  13.2 us
    reduce_sum x32, other arithmetic, single(): return jnp.sum(slope(member[None] - smooth_fc), axis=0)  10.1 us
    all_to_all x1, waiting for transfers between devices, body(): lax.all_to_all(sharp_derivative, 'ens', split_axis=0, concat_axis=1, tile...  9.81 us
  transfers between devices with their start and end apart: 15, of which 10 were waited for; matrix products, arithmetic and copies ran while one was open for 16% of the time, Pallas kernels for 0%

commit v1 on v0

v1 whole, which is shorter than its diff:
```python
import functools

import jax
import jax.numpy as jnp
import numpy as np
from jax import lax
from jax.experimental import pallas as pl
from jax.experimental.pallas import tpu as pltpu
from jax.sharding import PartitionSpec as P

MEMBERS, CHANNELS, ROWS, COLS = 16, 16, 128, 1440
BLOCKS = 8
BLOCK = COLS // BLOCKS
LANES, SIDE, HALO = 128, 64, 6
PAIRS = MEMBERS // 2
RC = 8
PAD = 8
SHARE = 0.95 / (MEMBERS - 1)
FINE = (0.5, 0.25)
COARSE = (20 / 64, 15 / 64, 6 / 64, 1 / 64)
VMEM = pl.BlockSpec(memory_space=pltpu.VMEM)
SMEM = pl.BlockSpec(memory_space=pltpu.SMEM)


def offset_of(block):
    return (BLOCK * block - HALO) % LANES


def lane_ids(shape=(RC, LANES)):
    return lax.broadcasted_iota(jnp.int32, shape, len(shape) - 1)


def column_runs(wanted):
    runs = []
    for lane, col in wanted:
        if runs:
            p, q, n = runs[-1]
            if p + n == lane and q + n == col and col % LANES:
                runs[-1] = (p, q, n + 1)
                continue
        runs.append((lane, col, 1))
    return runs


def gather_tile(load, parts, lanes):
    tile = None
    for source, p, q, n in parts:
        base = min(q // LANES * LANES, COLS - LANES)
        piece = load(source, base)
        shift = (p - (q - base)) % LANES
        if shift:
            piece = pltpu.roll(piece, shift, 1)
        tile = piece if tile is None else jnp.where((lanes >= p) & (lanes < p + n), piece, tile)
    return tile


def main_parts(source, block):
    o = offset_of(block)
    lanes = sorted(range(LANES), key=lambda j: (j + o) % LANES)
    runs = column_runs([((j + o) % LANES, (BLOCK * block - HALO + j) % COLS) for j in lanes])
    return [(source, p, q, n) for p, q, n in runs]


def side_parts(first, second, block):
    o = offset_of(block)
    parts = []
    for source, half in ((first, 0), (second, 1)):
        wanted = [
            ((r + o) % LANES, (BLOCK * block - HALO + LANES + r % SIDE) % COLS)
            for r in range(half * SIDE, (half + 1) * SIDE)
        ]
        parts += [(source, p, q, n) for p, q, n in column_runs(sorted(wanted))]
    return parts


def pack_kernel(x_ref, obs_ref, msg_ref, obs_msg_ref):
    lanes = lane_ids()

    def load_obs(source, base):
        return obs_ref[source, :, base : base + LANES]

    for h in range(2):
        for b in range(BLOCKS):
            obs_msg_ref[h * BLOCKS + b, 0] = gather_tile(load_obs, main_parts(h, b), lanes)
            obs_msg_ref[h * BLOCKS + b, 1] = gather_tile(load_obs, side_parts(h, h, b), lanes)

    def channel(c, carry):
        def load(source, base):
            return x_ref[source, c, :, base : base + LANES]

        for b in range(BLOCKS):
            dst = c * BLOCKS + b
            msg_ref[dst, 0] = gather_tile(load, main_parts(0, b), lanes)
            msg_ref[dst, 1] = gather_tile(load, main_parts(1, b), lanes)
            msg_ref[dst, 2] = gather_tile(load, side_parts(0, 1, b), lanes)
        return carry

    lax.fori_loop(0, CHANNELS, channel, 0)


def unpack_kernel(ret_ref, out_ref):
    lanes = lane_ids()

    def channel(c, carry):
        for m in range(2):
            for t in range((COLS + LANES - 1) // LANES):
                tile = None
                q = t * LANES
                end = min(q + LANES, COLS)
                while q < end:
                    b, k = q // BLOCK, q % BLOCK
                    stop = b * BLOCK + (BLOCK - SIDE if k < BLOCK - SIDE else BLOCK)
                    src = c * BLOCKS + b
                    if k < BLOCK - SIDE:
                        piece = ret_ref[src, m]
                    else:
                        piece = ret_ref[src, 2]
                        if m:
                            piece = pltpu.roll(piece, SIDE, 1)
                    p = q - t * LANES
                    tile = piece if tile is None else jnp.where(lanes >= p, piece, tile)
                    q = min(stop, end)
                if end - t * LANES == LANES:
                    out_ref[m, c, :, t * LANES : end] = tile
                else:
                    out_ref[m, c, :, t * LANES : end] = tile[:, : end - t * LANES]
        return carry

    lax.fori_loop(0, CHANNELS, channel, 0)


def taps(distance, weights):
    value = jnp.zeros(distance.shape, jnp.float32)
    for d, w in enumerate(weights):
        value = jnp.where(distance == d, w, value)
    return value


def matrices_kernel(o_ref, main_ref, side_ref, back_a_ref, back_b_ref, back_s_ref):
    o = o_ref[0]
    shape = (LANES, LANES)
    row = lax.broadcasted_iota(jnp.int32, shape, 0)
    col = lax.broadcasted_iota(jnp.int32, shape, 1)
    turned_row = (row - o) & (LANES - 1)
    turned_col = (col - o) & (LANES - 1)
    far = 99
    valid_col = (col >= 3) & (col < LANES - 3)
    valid_row = (row >= 3) & (row < LANES - 3)

    def put(ref, start, lane, distance, weights):
        tile = taps(distance, weights).astype(jnp.bfloat16)
        for i in range(3):
            ref[start + i * LANES : start + (i + 1) * LANES, lane : lane + LANES] = tile

    first_col = col < SIDE
    target_pair = jnp.where(first_col, col + (LANES - 3), col + (LANES - 3 - SIDE))
    first_turned = turned_row < SIDE
    source_side = jnp.where(first_turned, turned_row + LANES, turned_row + (LANES - SIDE))
    for s, weights in enumerate((FINE, COARSE)):
        lane = s * LANES
        put(main_ref, 0, lane, jnp.where(valid_col, jnp.abs(turned_row - col), far), weights)
        near = jnp.abs(turned_row - target_pair)
        put(side_ref, 0, lane, jnp.where(first_col, near, far), weights)
        same = first_turned == first_col
        put(side_ref, 3 * LANES, lane, jnp.where(same, jnp.abs(source_side - target_pair), far), weights)
        put(side_ref, 6 * LANES, lane, jnp.where(first_col, far, near), weights)

    out_main = (turned_col >= HALO) & (turned_col < LANES - HALO)
    out_second = (turned_col >= SIDE - HALO) & (turned_col < LANES - HALO)
    target_side = jnp.where(
        out_second, turned_col + SIDE, jnp.where(turned_col < SIDE, turned_col + LANES, turned_col)
    )
    row_first = row < SIDE
    source_pair = jnp.where(row_first, row + (LANES - 3), row + (LANES - 3 - SIDE))
    for s, weights in enumerate((FINE, COARSE)):
        start = s * 3 * LANES
        near = jnp.where(valid_row & out_main, jnp.abs(row - turned_col), far)
        cross = jnp.where(valid_row, jnp.abs(row - target_side), far)
        put(back_a_ref, start, 0, near, weights)
        put(back_a_ref, start, LANES, jnp.where(out_second, far, cross), weights)
        put(back_b_ref, start, 0, near, weights)
        put(back_b_ref, start, LANES, jnp.where(out_second, cross, far), weights)
        same = row_first == jnp.logical_not(out_second)
        put(back_s_ref, start, 0, jnp.where(same, jnp.abs(source_pair - target_side), far), weights)


def thirds(x):
    high = x.astype(jnp.bfloat16)
    rest = x - high.astype(jnp.float32)
    middle = rest.astype(jnp.bfloat16)
    low = (rest - middle.astype(jnp.float32)).astype(jnp.bfloat16)
    return [high, middle, low]


def times(parts, matrix):
    return jnp.dot(jnp.concatenate(parts, axis=1), matrix, preferred_element_type=jnp.float32)


def fine_rows(ref, i, start, size):
    at = lambda d: ref[i, pl.ds(start + PAD + d, size), :]
    return 0.25 * (at(-1) + at(1)) + 0.5 * at(0)


def coarse_rows(ref, i, start, size):
    at = lambda d: ref[i, pl.ds(start + PAD + d, size), :]
    return (
        (at(-3) + at(3)) * COARSE[3]
        + (at(-2) + at(2)) * COARSE[2]
        + (at(-1) + at(1)) * COARSE[1]
        + at(0) * COARSE[0]
    )


def mirror(ref, i):
    end = PAD + ROWS
    for outside, inside in ((PAD - 2, PAD), (PAD - 3, PAD + 1), (end + 1, end - 1), (end + 2, end - 2)):
        ref[i, outside : outside + 1, :] = -ref[i, inside : inside + 1, :]


def slope(d):
    return d * lax.rsqrt(d * d + 0.01)


def work_kernel(
    factor_ref, got_ref, obs_ref, lat_ref, main_ref, side_ref, back_a_ref, back_b_ref, back_s_ref,
    out_ref, fine_ref, coarse_ref, gfine_ref, gcoarse_ref,
):
    zeros = jnp.zeros((PAD, LANES), jnp.float32)

    def clear(i, carry):
        for ref in (fine_ref, coarse_ref):
            ref[i, 0:PAD, :] = zeros
            ref[i, PAD + ROWS : 2 * PAD + ROWS, :] = zeros
        return carry

    lax.fori_loop(0, 3 * PAIRS + 2, clear, 0)

    def clear_back(i, carry):
        for ref in (gfine_ref, gcoarse_ref):
            ref[i, 0:PAD, :] = zeros
            ref[i, PAD + ROWS : 2 * PAD + ROWS, :] = zeros
        return carry

    lax.fori_loop(0, 3 * PAIRS, clear_back, 0)

    def keep(i, both):
        fine_ref[i, PAD : PAD + ROWS, :] = both[:, :LANES]
        coarse_ref[i, PAD : PAD + ROWS, :] = both[:, LANES:]
        mirror(coarse_ref, i)

    def forward(p, carry):
        a, b, s = (thirds(got_ref[p, :, t].reshape(ROWS, LANES)) for t in range(3))
        keep(3 * p, times(a, main_ref[...]))
        keep(3 * p + 1, times(b, main_ref[...]))
        keep(3 * p + 2, times(a + s + b, side_ref[...]))
        return carry

    lax.fori_loop(0, PAIRS, forward, 0)
    a, s = (thirds(obs_ref[:, t].reshape(ROWS, LANES)) for t in range(2))
    keep(3 * PAIRS, times(a, main_ref[...]))
    keep(3 * PAIRS + 1, times(a + s + a, side_ref[...]))

    factor = factor_ref[0]

    def pull(n, carry):
        start = pl.multiple_of(n * RC, RC)
        weight = jnp.broadcast_to(lat_ref[pl.ds(start, RC), :] * factor, (RC, LANES))
        for rows, ref, gref in ((fine_rows, fine_ref, gfine_ref), (coarse_rows, coarse_ref, gcoarse_ref)):
            mains = [3 * (m // 2) + m % 2 for m in range(MEMBERS)]
            value = [rows(ref, i, start, RC) for i in mains]
            total = [None] * MEMBERS
            for m in range(MEMBERS):
                for k in range(m + 1, MEMBERS):
                    part = slope(value[m] - value[k])
                    total[m] = part if total[m] is None else total[m] + part
                    total[k] = -part if total[k] is None else total[k] - part
            target = rows(ref, 3 * PAIRS, start, RC)
            for m, i in enumerate(mains):
                grad = weight * (slope(value[m] - target) - SHARE * total[m])
                gref[i, pl.ds(start + PAD, RC), :] = grad

            value = [rows(ref, 3 * p + 2, start, RC) for p in range(PAIRS)]
            other = [pltpu.roll(v, SIDE, 1) for v in value]
            total = [slope(value[p] - other[p]) for p in range(PAIRS)]
            swapped = [None] * PAIRS
            for p in range(PAIRS):
                for k in range(p + 1, PAIRS):
                    part = slope(value[p] - value[k])
                    cross = slope(value[p] - other[k])
                    total[p] = total[p] + (part + cross)
                    total[k] = total[k] - part
                    swapped[k] = -cross if swapped[k] is None else swapped[k] - cross
            target = rows(ref, 3 * PAIRS + 1, start, RC)
            for p in range(PAIRS):
                full = total[p] if swapped[p] is None else total[p] + pltpu.roll(swapped[p], SIDE, 1)
                grad = weight * (slope(value[p] - target) - SHARE * full)
                gref[3 * p + 2, pl.ds(start + PAD, RC), :] = grad
        return carry

    lax.fori_loop(0, ROWS // RC, pull, 0)

    def backward(p, carry):
        def rows_of(i):
            mirror(gcoarse_ref, i)
            return thirds(fine_rows(gfine_ref, i, 0, ROWS)) + thirds(coarse_rows(gcoarse_ref, i, 0, ROWS))

        first = times(rows_of(3 * p), back_a_ref[...])
        second = times(rows_of(3 * p + 1), back_b_ref[...])
        side = times(rows_of(3 * p + 2), back_s_ref[...])
        blocks = (ROWS // RC, RC, LANES)
        out_ref[p, :, 0] = first[:, :LANES].reshape(blocks)
        out_ref[p, :, 1] = second[:, :LANES].reshape(blocks)
        out_ref[p, :, 2] = (side + first[:, LANES:] + second[:, LANES:]).reshape(blocks)
        return carry

    lax.fori_loop(0, PAIRS, backward, 0)


def shape(*dims, dtype=jnp.float32):
    return jax.ShapeDtypeStruct(dims, dtype)


def body(prediction_array, verifying_analysis, variable_penalty_factor):
    ens, lat = lax.axis_index("ens"), lax.axis_index("lat")
    block = lat % BLOCKS
    channel = 2 * ens + lat // BLOCKS
    offset = ((BLOCK * block - HALO) % LANES).astype(jnp.int32).reshape(1)
    factor = lax.dynamic_slice_in_dim(variable_penalty_factor, channel, 1)
    degrees = 0.25 * (np.arange(ROWS, dtype=np.float32) - (ROWS - 1) / 2.0)
    lat_weight = jnp.asarray(np.cos(np.deg2rad(degrees)).astype(np.float32)[:, None])

    msg, obs_msg = pl.pallas_call(
        pack_kernel,
        out_shape=(shape(128, 3, RC, LANES), shape(16, 2, RC, LANES)),
        in_specs=[VMEM, VMEM],
        out_specs=(VMEM, VMEM),
        name="pack",
    )(prediction_array, verifying_analysis)
    bf = jnp.bfloat16
    mats = pl.pallas_call(
        matrices_kernel,
        out_shape=(
            shape(3 * LANES, 2 * LANES, dtype=bf),
            shape(9 * LANES, 2 * LANES, dtype=bf),
            shape(6 * LANES, 2 * LANES, dtype=bf),
            shape(6 * LANES, 2 * LANES, dtype=bf),
            shape(6 * LANES, LANES, dtype=bf),
        ),
        in_specs=[SMEM],
        out_specs=(VMEM,) * 5,
        name="matrices",
        cost_estimate=pl.CostEstimate(flops=10_000_000, bytes_accessed=1_000_000, transcendentals=0),
    )(offset)
    obs_got = lax.all_to_all(obs_msg, "lat", 0, 0, tiled=True)
    got = lax.all_to_all(msg, ("ens", "lat"), 0, 0, tiled=True)
    padded = (ROWS + 2 * PAD, LANES)
    back = pl.pallas_call(
        work_kernel,
        out_shape=shape(PAIRS, ROWS // RC, 3, RC, LANES),
        in_specs=[SMEM] + [VMEM] * 8,
        out_specs=VMEM,
        scratch_shapes=[
            pltpu.VMEM((3 * PAIRS + 2, *padded), jnp.float32),
            pltpu.VMEM((3 * PAIRS + 2, *padded), jnp.float32),
            pltpu.VMEM((3 * PAIRS, *padded), jnp.float32),
            pltpu.VMEM((3 * PAIRS, *padded), jnp.float32),
        ],
        name="work",
    )(factor, got.reshape(PAIRS, ROWS // RC, 3, RC, LANES), obs_got, lat_weight, *mats)
    ret = lax.all_to_all(back.reshape(128, 3, RC, LANES), ("ens", "lat"), 0, 0, tiled=True)
    return pl.pallas_call(
        unpack_kernel,
        out_shape=shape(2, CHANNELS, RC, COLS),
        in_specs=[VMEM],
        out_specs=VMEM,
        name="unpack",
    )(ret)


def solution(mesh):
    placed = (P("ens", None, "lat", None), P("ens", "lat", None), P())
    return jax.shard_map(
        body, mesh=mesh, in_specs=placed, out_specs=P("ens", None, "lat", None), check_vma=False
    )
```

time: 201 us -> 104 us (0.52); the launches traced: 197 us -> 104 us
  starting transfers between devices: 50.2 us -> 5.55 us
  local copies, waits for them, and re-layouts: 40.8 us -> 1.7 us
  other arithmetic: 32.9 us -> 0 us
  Pallas kernels: 0 us -> 27.9 us
  waiting for transfers between devices: 50 us -> 22.4 us
  blocking collectives: 22.6 us -> 46.3 us
    ppermute x12 -> x0, starting transfers between devices: 35.3 us -> none  [the longest x6 22.1 us: with_halo(): lax.ppermute(lax.slice_in_dim(block, block.shape[dim] - width, None, axis...]
    pallas_call x0 -> x4, Pallas kernels: none -> 27.9 us  [the longest x1 17.7 us: body(): pl.pallas_call(work_kernel, out_shape=shape(PAIRS, ROWS // RC, 3, RC, LAN...]
    all_to_all x1 -> x2, blocking collectives: 22.6 us -> 46.3 us  [the longest x1 29.4 us: body(): lax.all_to_all(back.reshape(128, 3, RC, LANES), ('ens', 'lat'), 0, 0, til...]
    ppermute x12 -> x0, waiting for transfers between devices: 22.7 us -> none  [the longest x6 21.3 us: with_halo(): lax.ppermute(lax.slice_in_dim(block, 0, width, axis=dim), axis, backward)]
    dynamic_update_slice x32 -> x0, local copies, waits for them, and re-layouts: 20.9 us -> none  [couple_derivative(): pulls = lax.map(single, smooth_fc)]
    reduce_sum x32 -> x0, other arithmetic: 10.1 us -> none  [single(): return jnp.sum(slope(member[None] - smooth_fc), axis=0)]
    all_to_all x3 -> x1, starting transfers between devices: 14.9 us -> 5.55 us  [body(): got = lax.all_to_all(msg, ('ens', 'lat'), 0, 0, tiled=True)]
    select_n x5 -> x0, other arithmetic: 8.74 us -> none  [normal_kernel_smoother(): return jnp.where(inside[None, :, None], result, 0.0)]
  transfers between devices with their start and end apart: 15 -> 1, of which waited for: 10 -> 1; matrix products, arithmetic and copies ran while one was open for 16% -> 1% of each run, Pallas kernels for 0% -> 1%
where the time goes in v1:
time: 104 us
  blocking collectives  46.3 us (45%)
  Pallas kernels  27.9 us (27%)
  waiting for transfers between devices  22.4 us (22%)
  starting transfers between devices  5.55 us (5%)
  local copies, waits for them, and re-layouts  1.7 us (2%)
    all_to_all x1, blocking collectives, body(): lax.all_to_all(back.reshape(128, 3, RC, LANES), ('ens', 'lat'), 0, 0, til...  29.4 us
    all_to_all x1, waiting for transfers between devices, body(): got = lax.all_to_all(msg, ('ens', 'lat'), 0, 0, tiled=True)  22.4 us
    pallas_call x1, Pallas kernels, body(): pl.pallas_call(work_kernel, out_shape=shape(PAIRS, ROWS // RC, 3, RC, LAN...  17.7 us
    all_to_all x1, blocking collectives, body(): obs_got = lax.all_to_all(obs_msg, 'lat', 0, 0, tiled=True)  16.9 us
    all_to_all x1, starting transfers between devices, body(): got = lax.all_to_all(msg, ('ens', 'lat'), 0, 0, tiled=True)  5.55 us
    pallas_call x1, Pallas kernels, body(): pl.pallas_call(pack_kernel, out_shape=(shape(128, 3, RC, LANES), shape(16...  5.03 us
    pallas_call x1, Pallas kernels, body(): pl.pallas_call(unpack_kernel, out_shape=shape(2, CHANNELS, RC, COLS), in_...  3.87 us
  transfers between devices with their start and end apart: 1, of which 1 were waited for; matrix products, arithmetic and copies ran while one was open for 1% of the time, Pallas kernels for 1%

profile of v1, /device:TPU:1, one launch (start us, length us, event | category | flops | bytes accessed | tf_op | source)
XLA Modules:
  0.0 103.9 jit_solution(16324267408806600151)
XLA Ops:
  0.0 5.0 %pack.1 = (f32[128,3,8,128]{3,2,1,0:T(8,128)}, f32[16,2,8,128]{3,2,1,0:T(8,128)}) custom-call(f32[2,16,8,1440]{3,2,1,0:T(8,128)} %x_ref.1, f32[2,8,1440]{2,1,0:T(8,128)} %obs_ref.1), custom_call_target="tpu_custom_call" | custom-call | tf_op jit(solution)/shard_map/pack/pallas_call | solution.py:332
  5.0 16.9 %all_to_all.15.obs_ref = f32[16,2,8,128]{3,2,1,0:T(8,128)} all-to-all(f32[16,2,8,128]{3,2,1,0:T(8,128)} %get-tuple-element.13), channel_id=1, replica_groups=mesh['ens'=8,'lat'=16] {'lat'}, dimensions={0} | all-to-all | bytes 262144 | tf_op jit(solution)/shard_map/all_to_all | solution.py:354
  21.9 0.0 copy-start.1
  21.9 5.5 %all-to-all-start = ((f32[128,3,8,128]{3,2,1,0:T(8,128)}), f32[128,3,8,128]{3,2,1,0:T(8,128)S(1)}, u32[]{:S(2)}, u32[]{:S(2)}) async-start(f32[128,3,8,128]{3,2,1,0:T(8,128)} %get-tuple-element.12), calls=%async_computation | async-start | bytes 3145728 | tf_op jit(solution)/shard_map/all_to_all | solution.py:355
  27.5 0.0 copy-done.1
  27.5 0.6 dynamic_slice.3.factor_ref
  28.1 1.3 %matrices.1 = (bf16[384,256]{1,0:T(8,128)(2,1)}, bf16[1152,256]{1,0:T(8,128)(2,1)}, bf16[768,256]{1,0:T(8,128)(2,1)}, bf16[768,256]{1,0:T(8,128)(2,1)}, bf16[768,128]{1,0:T(8,128)(2,1)}) custom-call(s32[1]{0:T(128)} %bitcast.1.o_ref), custom_call_target="tpu_custom_call" | custom-call | flops 10000000 | bytes 1000000 | tf_op jit(solution)/shard_map/matrices/pallas_call | solution.py:340
  29.4 22.4 %all-to-all-done = f32[128,3,8,128]{3,2,1,0:T(8,128)S(1)} async-done(((f32[128,3,8,128]{3,2,1,0:T(8,128)}), f32[128,3,8,128]{3,2,1,0:T(8,128)S(1)}, u32[]{:S(2)}, u32[]{:S(2)}) %all-to-all-start) | async-done | bytes 1572896 | tf_op jit(solution)/shard_map/all_to_all | solution.py:355
  51.8 0.0 copy-start
  51.8 1.1 %copy-done = f32[128,3,8,128]{3,2,1,0:T(8,128)} copy-done((f32[128,3,8,128]{3,2,1,0:T(8,128)}, f32[128,3,8,128]{3,2,1,0:T(8,128)S(1)}, u32[]{:S(2)}) %copy-start) | copy-done | bytes 1572888
  52.9 17.7 %work.1 = f32[8,16,3,8,128]{4,3,2,1,0:T(8,128)} custom-call(f32[1]{0:T(128)} %dynamic_slice.3.factor_ref, f32[8,16,3,8,128]{4,3,2,1,0:T(8,128)} %bitcast.3, f32[16,2,8,128]{3,2,1,0:T(8,128)} %all_to_all.15.obs_ref, f32[128,1]{1,0:T(8,128)} %constant.57.clone.lat_ref, bf16[384,256]{1,0:T(8,128)(2,1)} %get-tuple-element.14.main_ref, ...), custom_call_target="tpu_custom_call" | custom-call | tf_op jit(solution)/shard_map/work/pallas_call | solution.py:357
  70.6 29.4 %all_to_all.16.ret_ref = f32[128,3,8,128]{3,2,1,0:T(8,128)} all-to-all(f32[128,3,8,128]{3,2,1,0:T(8,128)} %bitcast.4), channel_id=1, replica_groups=mesh['ens'=8,'lat'=16] {'ens','lat'}, dimensions={0} | all-to-all | bytes 3145728 | tf_op jit(solution)/shard_map/all_to_all | solution.py:370
  100.0 3.9 %unpack.1 = f32[2,16,8,1440]{3,2,1,0:T(8,128)} custom-call(f32[128,3,8,128]{3,2,1,0:T(8,128)} %all_to_all.16.ret_ref), custom_call_target="tpu_custom_call" | custom-call | tf_op jit(solution)/shard_map/unpack/pallas_call | solution.py:371
Async XLA Ops:
  21.9 5.6 %copy-start.1 = (f32[16]{0:T(128)S(1)}, f32[16]{0:T(128)}, u32[]{:S(2)}) copy-start(f32[16]{0:T(128)} %param.6) | copy-start | bytes 196
  21.9 29.9 %all-to-all-start = ((f32[128,3,8,128]{3,2,1,0:T(8,128)}), f32[128,3,8,128]{3,2,1,0:T(8,128)S(1)}, u32[]{:S(2)}, u32[]{:S(2)}) async-start(f32[128,3,8,128]{3,2,1,0:T(8,128)} %get-tuple-element.12), calls=%async_computation | async-start | bytes 3145728 | tf_op jit(solution)/shard_map/all_to_all | solution.py:355
  51.8 1.1 %copy-start = (f32[128,3,8,128]{3,2,1,0:T(8,128)}, f32[128,3,8,128]{3,2,1,0:T(8,128)S(1)}, u32[]{:S(2)}) copy-start(f32[128,3,8,128]{3,2,1,0:T(8,128)S(1)} %all-to-all-done) | copy-start | bytes 4718596

commit v2 on v1

v2 whole, which is shorter than its diff:
```python
import jax
import jax.numpy as jnp
import numpy as np
from jax import lax
from jax.experimental import pallas as pl
from jax.experimental.pallas import tpu as pltpu
from jax.sharding import PartitionSpec as P

MEMBERS, CHANNELS, ROWS, COLS = 16, 16, 128, 1440
BLOCKS = 8
BLOCK = COLS // BLOCKS
LANES, SIDE, HALO = 128, 64, 6
PAIRS = MEMBERS // 2
RC = 8
PAD = 8
LATS = 16
SHARE = 0.95 / (MEMBERS - 1)
FINE_SCALE, COARSE_SCALE = 16.0, 4096.0
VMEM = pl.BlockSpec(memory_space=pltpu.VMEM)
SMEM = pl.BlockSpec(memory_space=pltpu.SMEM)


def offset_of(block):
    return (BLOCK * block + LANES - HALO) % LANES


def lane_ids(shape=(RC, LANES)):
    return lax.broadcasted_iota(jnp.int32, shape, len(shape) - 1)


def column_runs(wanted):
    runs = []
    for lane, col in wanted:
        if runs:
            p, q, n = runs[-1]
            if p + n == lane and q + n == col and col % LANES:
                runs[-1] = (p, q, n + 1)
                continue
        runs.append((lane, col, 1))
    return runs


def gather_tile(load, parts, lanes):
    tile = None
    for source, p, q, n in parts:
        base = min(q // LANES * LANES, COLS - LANES)
        piece = load(source, base)
        shift = (p - (q - base)) % LANES
        if shift:
            piece = pltpu.roll(piece, shift, 1)
        tile = piece if tile is None else jnp.where((lanes >= p) & (lanes < p + n), piece, tile)
    return tile


def main_parts(source, block):
    o = offset_of(block)
    lanes = sorted(range(LANES), key=lambda j: (j + o) % LANES)
    runs = column_runs([((j + o) % LANES, (BLOCK * block - HALO + j) % COLS) for j in lanes])
    return [(source, p, q, n) for p, q, n in runs]


def side_parts(first, second, block):
    o = offset_of(block)
    parts = []
    for source, half in ((first, 0), (second, 1)):
        wanted = [
            ((r + o) % LANES, (BLOCK * block - HALO + LANES + r % SIDE) % COLS)
            for r in range(half * SIDE, (half + 1) * SIDE)
        ]
        parts += [(source, p, q, n) for p, q, n in column_runs(sorted(wanted))]
    return parts


def pack_obs_kernel(lat_ref, obs_ref, obs_msg_ref):
    lanes = lane_ids()
    me = lat_ref[0]

    def load_obs(source, base):
        return obs_ref[source, :, base : base + LANES]

    for h in range(2):
        for b in range(BLOCKS):
            slot = me ^ (h * BLOCKS + b)
            obs_msg_ref[slot, 0] = gather_tile(load_obs, main_parts(h, b), lanes)
            obs_msg_ref[slot, 1] = gather_tile(load_obs, side_parts(h, h, b), lanes)


def pack_kernel(x_ref, msg_ref):
    lanes = lane_ids()

    def channel(c, carry):
        def load(source, base):
            return x_ref[source, c, :, base : base + LANES]

        for b in range(BLOCKS):
            dst = c * BLOCKS + b
            msg_ref[dst, 0] = gather_tile(load, main_parts(0, b), lanes)
            msg_ref[dst, 1] = gather_tile(load, main_parts(1, b), lanes)
            msg_ref[dst, 2] = gather_tile(load, side_parts(0, 1, b), lanes)
        return carry

    lax.fori_loop(0, x_ref.shape[1], channel, 0)


def unpack_kernel(ret_ref, out_ref):
    lanes = lane_ids()

    def channel(c, carry):
        for m in range(2):
            for t in range((COLS + LANES - 1) // LANES):
                tile = None
                q = t * LANES
                end = min(q + LANES, COLS)
                while q < end:
                    b, k = q // BLOCK, q % BLOCK
                    stop = b * BLOCK + (BLOCK - SIDE if k < BLOCK - SIDE else BLOCK)
                    src = c * BLOCKS + b
                    if k < BLOCK - SIDE:
                        piece = ret_ref[src, m]
                    else:
                        piece = ret_ref[src, 2]
                        if m:
                            piece = pltpu.roll(piece, SIDE, 1)
                    p = q - t * LANES
                    tile = piece if tile is None else jnp.where(lanes >= p, piece, tile)
                    q = min(stop, end)
                if end - t * LANES == LANES:
                    out_ref[m, c, :, t * LANES : end] = tile
                else:
                    out_ref[m, c, :, t * LANES : end] = tile[:, : end - t * LANES]
        return carry

    lax.fori_loop(0, out_ref.shape[1], channel, 0)


def along_lon(x):
    t = x + pltpu.roll(x, 1, 1)
    return t + pltpu.roll(t, LANES - 1, 1)


def along_lat(x, ref, i):
    ref[i, PAD : PAD + ROWS, :] = x
    return (ref[i, PAD - 1 : PAD - 1 + ROWS, :] + ref[i, PAD + 1 : PAD + 1 + ROWS, :]) + (x + x)


def slope(d, floor):
    return d * lax.rsqrt(d * d + floor)


def work_kernel(
    ens_ref, lat_ref, factor_ref, weight_ref, got_ref, obs_ref,
    out_ref, fine_ref, coarse_ref, gfine_ref, gcoarse_ref, rows_ref,
):
    me = lat_ref[0]
    block = me & (BLOCKS - 1)
    factor = factor_ref[2 * ens_ref[0] + (me >> 3)]
    offset = BLOCK * block + LANES - HALO
    turned = (lane_ids((ROWS, LANES)) - offset) & (LANES - 1)
    upper = turned >= SIDE
    inner = (turned >= LANES - 3) | (turned < SIDE - 3)
    outer = (turned >= LANES - HALO) | (turned < SIDE - HALO)
    zeros = jnp.zeros((PAD, LANES), jnp.float32)
    for i in range(rows_ref.shape[0]):
        rows_ref[i, 0:PAD, :] = zeros
        rows_ref[i, PAD + ROWS : 2 * PAD + ROWS, :] = zeros

    def both_scales(x, i):
        fine = along_lat(along_lon(x), rows_ref, 3 * i)
        twice = along_lat(along_lon(fine), rows_ref, 3 * i + 1)
        return fine, along_lat(along_lon(twice), rows_ref, 3 * i + 2)

    def join(a, b):
        return jnp.where(inner, a, pltpu.roll(b, SIDE, 1))

    def forward(p, carry):
        a, b, s = (got_ref[p, :, t].reshape(ROWS, LANES) for t in range(3))
        first = both_scales(a, 0)
        second = both_scales(b, 1)
        side_a = both_scales(jnp.where(upper, a, s), 2)
        side_b = both_scales(jnp.where(upper, b, pltpu.roll(s, SIDE, 1)), 3)
        for s, ref in enumerate((fine_ref, coarse_ref)):
            ref[3 * p] = first[s]
            ref[3 * p + 1] = second[s]
            ref[3 * p + 2] = join(side_a[s], side_b[s])
        return carry

    lax.fori_loop(0, PAIRS, forward, 0)
    a, s = (
        jnp.concatenate([obs_ref[me ^ l, t] for l in range(LATS)], axis=0) for t in range(2)
    )
    first = both_scales(a, 0)
    side = both_scales(jnp.where(upper, a, s), 1)
    for s, ref in enumerate((fine_ref, coarse_ref)):
        ref[3 * PAIRS] = first[s]
        ref[3 * PAIRS + 1] = join(side[s], side[s])

    def pull(n, carry):
        start = pl.multiple_of(n * RC, RC)
        here = pl.ds(start, RC)
        row_weight = jnp.broadcast_to(weight_ref[here, :] * factor, (RC, LANES))
        for ref, gref, scale in ((fine_ref, gfine_ref, FINE_SCALE), (coarse_ref, gcoarse_ref, COARSE_SCALE)):
            floor = 0.01 * scale * scale
            weight = row_weight * (1.0 / scale)
            shared = weight * SHARE
            mains = [3 * (m // 2) + m % 2 for m in range(MEMBERS)]
            value = [ref[i, here, :] for i in mains]
            total = [None] * MEMBERS
            for m in range(MEMBERS):
                for k in range(m + 1, MEMBERS):
                    part = slope(value[m] - value[k], floor)
                    total[m] = part if total[m] is None else total[m] + part
                    total[k] = -part if total[k] is None else total[k] - part
            target = ref[3 * PAIRS, here, :]
            for m, i in enumerate(mains):
                gref[i, here, :] = weight * slope(value[m] - target, floor) - shared * total[m]

            value = [ref[3 * p + 2, here, :] for p in range(PAIRS)]
            other = [pltpu.roll(v, SIDE, 1) for v in value]
            total = [slope(value[p] - other[p], floor) for p in range(PAIRS)]
            swapped = [None] * PAIRS
            for p in range(PAIRS):
                for k in range(p + 1, PAIRS):
                    part = slope(value[p] - value[k], floor)
                    cross = slope(value[p] - other[k], floor)
                    total[p] = total[p] + (part + cross)
                    total[k] = total[k] - part
                    swapped[k] = -cross if swapped[k] is None else swapped[k] - cross
            target = ref[3 * PAIRS + 1, here, :]
            for p in range(PAIRS):
                full = total[p] if swapped[p] is None else total[p] + pltpu.roll(swapped[p], SIDE, 1)
                gref[3 * p + 2, here, :] = weight * slope(value[p] - target, floor) - shared * full
        return carry

    lax.fori_loop(0, ROWS // RC, pull, 0)

    def adjoint(fine, coarse, i):
        once = along_lat(along_lon(coarse), rows_ref, 3 * i)
        twice = along_lat(along_lon(once), rows_ref, 3 * i + 1)
        return along_lat(along_lon(twice + fine), rows_ref, 3 * i + 2)

    def backward(p, carry):
        def split(ref):
            a, b, s = ref[3 * p], ref[3 * p + 1], ref[3 * p + 2]
            return a, b, jnp.where(inner, s, a), jnp.where(inner, pltpu.roll(s, SIDE, 1), b)

        a, b, side_a, side_b = (
            adjoint(f, c, i) for i, (f, c) in enumerate(zip(split(gfine_ref), split(gcoarse_ref)))
        )
        blocks = (ROWS // RC, RC, LANES)
        out_ref[p, :, 0] = a.reshape(blocks)
        out_ref[p, :, 1] = b.reshape(blocks)
        out_ref[p, :, 2] = jnp.where(outer, side_a, pltpu.roll(side_b, SIDE, 1)).reshape(blocks)
        return carry

    lax.fori_loop(0, PAIRS, backward, 0)


def shape(*dims):
    return jax.ShapeDtypeStruct(dims, jnp.float32)


def grant(mib):
    return pltpu.CompilerParams(vmem_limit_bytes=mib << 20)


def exchange_slots(slots):
    slots = slots.reshape(2, 2, 2, 2, *slots.shape[1:])
    for axis in range(4):
        step = 8 >> axis
        kept = lax.index_in_dim(slots, 0, axis, keepdims=True)
        sent = lax.index_in_dim(slots, 1, axis, keepdims=True)
        got = lax.ppermute(sent, "lat", [(i, i ^ step) for i in range(LATS)])
        slots = jnp.concatenate([kept, got], axis=axis)
    return slots.reshape(LATS, *slots.shape[4:])


def body(prediction_array, verifying_analysis, variable_penalty_factor):
    ens = lax.axis_index("ens").astype(jnp.int32).reshape(1)
    lat = lax.axis_index("lat").astype(jnp.int32).reshape(1)
    degrees = 0.25 * (np.arange(ROWS, dtype=np.float32) - (ROWS - 1) / 2.0)
    lat_weight = jnp.asarray(np.cos(np.deg2rad(degrees)).astype(np.float32)[:, None])

    msg = pl.pallas_call(
        pack_kernel,
        out_shape=shape(128, 3, RC, LANES),
        in_specs=[VMEM],
        out_specs=VMEM,
        compiler_params=grant(8),
        name="pack",
    )(prediction_array)
    got = lax.all_to_all(msg, ("ens", "lat"), 0, 0, tiled=True)
    obs_msg = pl.pallas_call(
        pack_obs_kernel,
        out_shape=shape(LATS, 2, RC, LANES),
        in_specs=[SMEM, VMEM],
        out_specs=VMEM,
        compiler_params=grant(2),
        name="pack_obs",
    )(lat, verifying_analysis)
    obs_got = exchange_slots(obs_msg)
    padded = (ROWS + 2 * PAD, LANES)
    back = pl.pallas_call(
        work_kernel,
        out_shape=shape(PAIRS, ROWS // RC, 3, RC, LANES),
        in_specs=[SMEM, SMEM, SMEM, VMEM, VMEM, VMEM],
        out_specs=VMEM,
        scratch_shapes=[
            pltpu.VMEM((3 * PAIRS + 2, ROWS, LANES), jnp.float32),
            pltpu.VMEM((3 * PAIRS + 2, ROWS, LANES), jnp.float32),
            pltpu.VMEM((3 * PAIRS, ROWS, LANES), jnp.float32),
            pltpu.VMEM((3 * PAIRS, ROWS, LANES), jnp.float32),
            pltpu.VMEM((12, *padded), jnp.float32),
        ],
        compiler_params=grant(16),
        name="work",
    )(ens, lat, variable_penalty_factor, lat_weight, got.reshape(PAIRS, ROWS // RC, 3, RC, LANES), obs_got)
    ret = lax.all_to_all(back.reshape(128, 3, RC, LANES), ("ens", "lat"), 0, 0, tiled=True)
    return pl.pallas_call(
        unpack_kernel,
        out_shape=shape(2, CHANNELS, RC, COLS),
        in_specs=[VMEM],
        out_specs=VMEM,
        compiler_params=grant(8),
        name="unpack",
    )(ret)


def solution(mesh):
    placed = (P("ens", None, "lat", None), P("ens", "lat", None), P())
    return jax.shard_map(
        body, mesh=mesh, in_specs=placed, out_specs=P("ens", None, "lat", None), check_vma=False
    )
```

time: 104 us -> 107 us (1.029)
  starting transfers between devices: 5.55 us -> 21.2 us
  blocking collectives: 46.3 us -> 31.9 us
    ppermute x0 -> x4, waiting for transfers between devices: none -> 23.4 us  [exchange_slots(): got = lax.ppermute(sent, 'lat', [(i, i ^ step) for i in range(LATS)])]
    all_to_all x1, waiting for transfers between devices: 22.4 us -> 0.01 us  [body(): got = lax.all_to_all(msg, ('ens', 'lat'), 0, 0, tiled=True)]
    all_to_all x1 -> x0, blocking collectives: 16.9 us -> none  [body(): obs_got = lax.all_to_all(obs_msg, 'lat', 0, 0, tiled=True)]
    ppermute x0 -> x4, starting transfers between devices: none -> 9.69 us  [exchange_slots(): got = lax.ppermute(sent, 'lat', [(i, i ^ step) for i in range(LATS)])]
    all_to_all x1, starting transfers between devices: 5.55 us -> 11.5 us  [body(): got = lax.all_to_all(msg, ('ens', 'lat'), 0, 0, tiled=True)]
    pallas_call x1, Pallas kernels: 17.7 us -> 22.2 us  [body(): pl.pallas_call(work_kernel, out_shape=shape(PAIRS, ROWS // RC, 3, RC, LAN...]
    pallas_call x2, Pallas kernels: 6.37 us -> 3.62 us  [the longest x1 3.48 us: body(): pl.pallas_call(pack_kernel, out_shape=shape(128, 3, RC, LANES), in_specs=...]
    all_to_all x1, blocking collectives: 29.4 us -> 31.9 us  [body(): lax.all_to_all(back.reshape(128, 3, RC, LANES), ('ens', 'lat'), 0, 0, til...]
  transfers between devices with their start and end apart: 1 -> 5, of which waited for: 1 -> 4; matrix products, arithmetic and copies ran while one was open for 1% -> 0% of each run, Pallas kernels for 1% -> 0%
where the time goes in v2:
time: 107 us; the launch traced here: 106 us
  blocking collectives  31.9 us (30%)
  Pallas kernels  28.3 us (26%)
  waiting for transfers between devices  23.4 us (22%)
  starting transfers between devices  21.2 us (20%)
  local copies, waits for them, and re-layouts  1.43 us (1%)
    all_to_all x1, blocking collectives, body(): lax.all_to_all(back.reshape(128, 3, RC, LANES), ('ens', 'lat'), 0, 0, til...  31.9 us
    ppermute x4, waiting for transfers between devices, exchange_slots(): got = lax.ppermute(sent, 'lat', [(i, i ^ step) for i in range(LATS)])  23.4 us
    pallas_call x1, Pallas kernels, body(): pl.pallas_call(work_kernel, out_shape=shape(PAIRS, ROWS // RC, 3, RC, LAN...  22.2 us
    all_to_all x1, starting transfers between devices, body(): got = lax.all_to_all(msg, ('ens', 'lat'), 0, 0, tiled=True)  11.5 us
    ppermute x4, starting transfers between devices, exchange_slots(): got = lax.ppermute(sent, 'lat', [(i, i ^ step) for i in range(LATS)])  9.69 us
    pallas_call x1, Pallas kernels, body(): pl.pallas_call(pack_kernel, out_shape=shape(128, 3, RC, LANES), in_specs=...  3.48 us
    pallas_call x1, Pallas kernels, body(): pl.pallas_call(unpack_kernel, out_shape=shape(2, CHANNELS, RC, COLS), in_...  2.47 us
  transfers between devices with their start and end apart: 5, of which 4 were waited for; matrix products, arithmetic and copies ran while one was open for 0% of the time, Pallas kernels for 0%

profile of v2, /device:TPU:1, one launch (start us, length us, event | category | flops | bytes accessed | tf_op | source)
XLA Modules:
  0.0 106.3 jit_solution(5726195268949175445)
XLA Ops:
  0.0 0.0 copy-start
  0.0 1.4 %copy-done = f32[2,16,8,1440]{3,2,1,0:T(8,128)S(1)} copy-done((f32[2,16,8,1440]{3,2,1,0:T(8,128)S(1)}, f32[2,16,8,1440]{3,2,1,0:T(8,128)}, u32[]{:S(2)}) %copy-start) | copy-done | bytes 1474584
  1.4 3.5 %pack.1 = f32[128,3,8,128]{3,2,1,0:T(8,128)} custom-call(f32[2,16,8,1440]{3,2,1,0:T(8,128)S(1)} %copy-done), custom_call_target="tpu_custom_call" | custom-call | tf_op jit(solution)/shard_map/pack/pallas_call | solution.py:283
  4.9 0.0 copy-start.1
  4.9 11.5 %all-to-all-start = ((f32[128,3,8,128]{3,2,1,0:T(8,128)}), f32[128,3,8,128]{3,2,1,0:T(8,128)S(1)}, u32[]{:S(2)}, u32[]{:S(2)}) async-start(f32[128,3,8,128]{3,2,1,0:T(8,128)} %pack.1), calls=%async_computation | async-start | bytes 3145728 | tf_op jit(solution)/shard_map/all_to_all | solution.py:291
  16.4 0.0 copy-start.2
  16.4 0.0 copy-start.3
  16.4 0.0 copy-done.1
  16.4 0.1 pack_obs.1
  16.6 2.9 %collective-permute-start = (f32[1,2,2,2,2,8,128]{6,5,4,3,2,1,0:T(8,128)S(1)}, f32[1,2,2,2,2,8,128]{6,5,4,3,2,1,0:T(8,128)S(1)}, u32[]{:S(2)}, u32[]{:S(2)}) collective-permute-start(f32[1,2,2,2,2,8,128]{6,5,4,3,2,1,0:T(8,128)S(1)} %bitcast.11), channel_id=1, source_target_pairs={{0,8},{1,9},{2,10},{3,11},{4,12},{5,13},{6,14},{7,15},{8,0},{9,1},... | collective-permute-start | bytes 196616 | tf_op jit(solution)/shard_map/ppermute | solution.py:272
  19.5 18.0 %collective-permute-done = f32[1,2,2,2,2,8,128]{6,5,4,3,2,1,0:T(8,128)S(1)} collective-permute-done((f32[1,2,2,2,2,8,128]{6,5,4,3,2,1,0:T(8,128)S(1)}, f32[1,2,2,2,2,8,128]{6,5,4,3,2,1,0:T(8,128)S(1)}, u32[]{:S(2)}, u32[]{:S(2)}) %collective-permute-start) | collective-permute-done | bytes 65568 | tf_op jit(solution)/shard_map/ppermute | solution.py:272
  37.5 0.4 collective-permute-start.1
  37.9 2.8 %collective-permute-done.1 = f32[2,1,2,2,2,8,128]{6,5,4,3,2,1,0:T(8,128)S(1)} collective-permute-done((f32[2,1,2,2,2,8,128]{6,5,4,3,2,1,0:T(8,128)S(1)}, f32[2,1,2,2,2,8,128]{6,5,4,3,2,1,0:T(8,128)S(1)}, u32[]{:S(2)}, u32[]{:S(2)}) %collective-permute-start.1) | collective-permute-done | bytes 65568 | tf_op jit(solution)/shard_map/ppermute | solution.py:272
  40.7 3.2 %collective-permute-start.2 = (f32[2,2,1,2,2,8,128]{6,5,4,3,2,1,0:T(8,128)S(1)}, f32[2,2,1,2,2,8,128]{6,5,4,3,2,1,0:T(8,128)S(1)}, u32[]{:S(2)}, u32[]{:S(2)}) collective-permute-start(f32[2,2,1,2,2,8,128]{6,5,4,3,2,1,0:T(8,128)S(1)} %get-tuple-element.8), channel_id=1, source_target_pairs={{0,2},{1,3},{2,0},{3,1},{4,6},{5,7},{6,4},{7,5},{8,10},{9,11},{10,... | collective-permute-start | bytes 196616 | tf_op jit(solution)/shard_map/ppermute | solution.py:272
  43.9 1.7 %collective-permute-done.2 = f32[2,2,1,2,2,8,128]{6,5,4,3,2,1,0:T(8,128)S(1)} collective-permute-done((f32[2,2,1,2,2,8,128]{6,5,4,3,2,1,0:T(8,128)S(1)}, f32[2,2,1,2,2,8,128]{6,5,4,3,2,1,0:T(8,128)S(1)}, u32[]{:S(2)}, u32[]{:S(2)}) %collective-permute-start.2) | collective-permute-done | bytes 65568 | tf_op jit(solution)/shard_map/ppermute | solution.py:272
  45.6 3.2 %collective-permute-start.3 = (f32[2,2,2,1,2,8,128]{6,5,4,3,2,1,0:T(8,128)S(1)}, f32[2,2,2,1,2,8,128]{6,5,4,3,2,1,0:T(8,128)S(1)}, u32[]{:S(2)}, u32[]{:S(2)}) collective-permute-start(f32[2,2,2,1,2,8,128]{6,5,4,3,2,1,0:T(8,128)S(1)} %get-tuple-element.6), channel_id=1, source_target_pairs={{0,1},{1,0},{2,3},{3,2},{4,5},{5,4},{6,7},{7,6},{8,9},{9,8},{10,11... | collective-permute-start | bytes 196616 | tf_op jit(solution)/shard_map/ppermute | solution.py:272
  48.8 0.9 collective-permute-done.3
  49.7 0.0 all-to-all-done
  49.7 0.0 copy-done.2
  49.7 0.0 copy-done.3
  49.7 22.2 %work.1 = f32[8,16,3,8,128]{4,3,2,1,0:T(8,128)S(1)} custom-call(s32[1]{0:T(128)} %bitcast.ens_ref, s32[1]{0:T(128)} %bitcast.1.lat_ref, f32[16]{0:T(128)S(1)} %copy-done.3, f32[128,1]{1,0:T(8,128)S(1)} %copy-done.2, f32[8,16,3,8,128]{4,3,2,1,0:T(8,128)S(1)} %bitcast.7, f32[16,2,8,128]{3,2,1,0:T(8,128)S(1)} %bitcast.9), custom_call_target="tpu_custom_call" | custom-call | tf_op jit(solution)/shard_map/work/pallas_call | solution.py:302
  72.0 31.9 %all_to_all.10.ret_ref = f32[128,3,8,128]{3,2,1,0:T(8,128)S(1)} all-to-all(f32[128,3,8,128]{3,2,1,0:T(8,128)S(1)} %bitcast.8), channel_id=1, replica_groups=mesh['ens'=8,'lat'=16] {'ens','lat'}, dimensions={0} | all-to-all | bytes 3145728 | tf_op jit(solution)/shard_map/all_to_all | solution.py:317
  103.8 2.5 %unpack.1 = f32[2,16,8,1440]{3,2,1,0:T(8,128)} custom-call(f32[128,3,8,128]{3,2,1,0:T(8,128)S(1)} %all_to_all.10.ret_ref), custom_call_target="tpu_custom_call" | custom-call | tf_op jit(solution)/shard_map/unpack/pallas_call | solution.py:318
  (5 shorter events, 0.0 us)
Async XLA Ops:
  0.0 1.4 %copy-start = (f32[2,16,8,1440]{3,2,1,0:T(8,128)S(1)}, f32[2,16,8,1440]{3,2,1,0:T(8,128)}, u32[]{:S(2)}) copy-start(f32[2,16,8,1440]{3,2,1,0:T(8,128)} %x_ref.1) | copy-start | bytes 4423684
  4.9 11.5 %copy-start.1 = (f32[2,8,1440]{2,1,0:T(8,128)S(1)}, f32[2,8,1440]{2,1,0:T(8,128)}, u32[]{:S(2)}) copy-start(f32[2,8,1440]{2,1,0:T(8,128)} %obs_ref.1) | copy-start | bytes 276484
  4.9 44.8 %all-to-all-start = ((f32[128,3,8,128]{3,2,1,0:T(8,128)}), f32[128,3,8,128]{3,2,1,0:T(8,128)S(1)}, u32[]{:S(2)}, u32[]{:S(2)}) async-start(f32[128,3,8,128]{3,2,1,0:T(8,128)} %pack.1), calls=%async_computation | async-start | bytes 3145728 | tf_op jit(solution)/shard_map/all_to_all | solution.py:291
  16.4 33.3 %copy-start.2 = (f32[128,1]{1,0:T(8,128)S(1)}, f32[128,1]{1,0:T(8,128)}, u32[]{:S(2)}) copy-start(f32[128,1]{1,0:T(8,128)} %constant.11.clone.weight_ref) | copy-start | bytes 1540
  16.4 33.3 %copy-start.3 = (f32[16]{0:T(128)S(1)}, f32[16]{0:T(128)}, u32[]{:S(2)}) copy-start(f32[16]{0:T(128)} %factor_ref.1) | copy-start | bytes 196
  16.6 20.9 %collective-permute-start = (f32[1,2,2,2,2,8,128]{6,5,4,3,2,1,0:T(8,128)S(1)}, f32[1,2,2,2,2,8,128]{6,5,4,3,2,1,0:T(8,128)S(1)}, u32[]{:S(2)}, u32[]{:S(2)}) collective-permute-start(f32[1,2,2,2,2,8,128]{6,5,4,3,2,1,0:T(8,128)S(1)} %bitcast.11), channel_id=1, source_target_pairs={{0,8},{1,9},{2,10},{3,11},{4,12},{5,13},{6,14},{7,15},{8,0},{9,1},... | collective-permute-start | bytes 196616 | tf_op jit(solution)/shard_map/ppermute | solution.py:272
  37.5 3.2 %collective-permute-start.1 = (f32[2,1,2,2,2,8,128]{6,5,4,3,2,1,0:T(8,128)S(1)}, f32[2,1,2,2,2,8,128]{6,5,4,3,2,1,0:T(8,128)S(1)}, u32[]{:S(2)}, u32[]{:S(2)}) collective-permute-start(f32[2,1,2,2,2,8,128]{6,5,4,3,2,1,0:T(8,128)S(1)} %get-tuple-element.10), channel_id=1, source_target_pairs={{0,4},{1,5},{2,6},{3,7},{4,0},{5,1},{6,2},{7,3},{8,12},{9,13},{10,... | collective-permute-start | bytes 196616 | tf_op jit(solution)/shard_map/ppermute | solution.py:272
  40.7 4.9 %collective-permute-start.2 = (f32[2,2,1,2,2,8,128]{6,5,4,3,2,1,0:T(8,128)S(1)}, f32[2,2,1,2,2,8,128]{6,5,4,3,2,1,0:T(8,128)S(1)}, u32[]{:S(2)}, u32[]{:S(2)}) collective-permute-start(f32[2,2,1,2,2,8,128]{6,5,4,3,2,1,0:T(8,128)S(1)} %get-tuple-element.8), channel_id=1, source_target_pairs={{0,2},{1,3},{2,0},{3,1},{4,6},{5,7},{6,4},{7,5},{8,10},{9,11},{10,... | collective-permute-start | bytes 196616 | tf_op jit(solution)/shard_map/ppermute | solution.py:272
  45.6 4.1 %collective-permute-start.3 = (f32[2,2,2,1,2,8,128]{6,5,4,3,2,1,0:T(8,128)S(1)}, f32[2,2,2,1,2,8,128]{6,5,4,3,2,1,0:T(8,128)S(1)}, u32[]{:S(2)}, u32[]{:S(2)}) collective-permute-start(f32[2,2,2,1,2,8,128]{6,5,4,3,2,1,0:T(8,128)S(1)} %get-tuple-element.6), channel_id=1, source_target_pairs={{0,1},{1,0},{2,3},{3,2},{4,5},{5,4},{6,7},{7,6},{8,9},{9,8},{10,11... | collective-permute-start | bytes 196616 | tf_op jit(solution)/shard_map/ppermute | solution.py:272
